TPU v7x, 32 devices: a whole 2x2x4 slice. The times are simulated.
32 devices in a mesh: section: 4 (over x, core), dp: 8 (over z, y).
Axes of the slice: x: 2, y: 2, z: 4, core: 2. Of those that a mesh axis runs over, the one named last changes fastest.
Arguments:
- latent_states: bfloat16 [4, 32, 96, 2048], P('section', 'dp'), may hold values from -8 to 8
- rescale_factor: float32 [2048], replicated, may hold values from 0.25 to 1.75
- embedding_matrix: bfloat16 [2048, 128], P('section'), may hold values from -0.125 to 0.125
- request_span: int32 [4, 32], replicated, may hold values from 8 to 32
- passage_span: int32 [4, 32], replicated, may hold values from 32 to 64
- matching_pair: int32 [4, 32], replicated, may hold values from 0 to 31, each once within a row
- steepness_pair: float32 [2], replicated, may hold values from 8 to 400
Outputs:
- grad_hidden: bfloat16 [4, 32, 96, 2048], P('section', 'dp')
- pair_loss: float32 [4, 32], P('section', 'dp')
Inputs may be any that keep to these rules, and one draw needn't show every extreme that they name: Each matching_pair[m] names every pair of the micro-batch once.
All inputs are finite; a program needn't handle non-finite values.
Results may differ from a plain program's by a relative error of at most 0.006.
The roundings to bfloat16 on the way count: a program that leaves them out, or rounds other values in their place, can miss the bound.
Values may be sent and summed in bfloat16 or wider, within the bound.
A program may use at most 64 MiB of HBM per device.

v0:
```python
import math
import jax
import jax.numpy as jnp
from jax import lax
from jax.sharding import PartitionSpec as P

QLEN = 32
DLEN = 64
EPSILON = 1e-06
OBJECTIVE_FACTOR = 1024.0
MASKED = -1e30


def head_forward(token_rows, rescale_factor, embedding_matrix):
    values = token_rows.astype(jnp.float32)
    inverse_rms = lax.rsqrt(jnp.mean(values * values, axis=-1, keepdims=True) + EPSILON)
    normed = (values * inverse_rms * rescale_factor).astype(jnp.bfloat16)
    projected = jnp.dot(normed, embedding_matrix, preferred_element_type=jnp.float32)
    inverse_length = lax.rsqrt(jnp.sum(projected * projected, axis=-1, keepdims=True) + EPSILON)
    vectors = (projected * inverse_length).astype(jnp.bfloat16)
    return (vectors, projected, inverse_length, inverse_rms)


def head_backward(
    token_rows,
    rescale_factor,
    embedding_matrix,
    projected,
    inverse_length,
    inverse_rms,
    grad_vectors,
):
    unit = projected * inverse_length
    along = jnp.sum(unit * grad_vectors, axis=-1, keepdims=True)
    grad_projected = (inverse_length * (grad_vectors - unit * along)).astype(jnp.bfloat16)
    grad_normed = lax.dot_general(
        grad_projected,
        embedding_matrix,
        (((1,), (1,)), ((), ())),
        preferred_element_type=jnp.float32,
    )
    values = token_rows.astype(jnp.float32)
    weighted = grad_normed * rescale_factor
    mean_term = jnp.mean(values * weighted, axis=-1, keepdims=True)
    grad_rows = (
        inverse_rms * weighted - values * (inverse_rms * inverse_rms * inverse_rms) * mean_term
    )
    return grad_rows.astype(jnp.bfloat16)


def pool_tokens(similarity, pooling_steepness, live):
    scaled = jnp.where(live[None], pooling_steepness * similarity, MASKED)
    highest = jnp.max(scaled, axis=2, keepdims=True)
    exponent = jnp.exp(scaled - highest)
    totals = jnp.sum(exponent, axis=2, keepdims=True)
    smooth = (highest[:, :, 0] + jnp.log(totals[:, :, 0])) / pooling_steepness
    return (smooth, exponent / totals)


def versus_term(relevance_matrix, matching_pair, logit_multiplier):
    unnormalized_odds = logit_multiplier * relevance_matrix
    highest = jnp.max(unnormalized_odds, axis=1, keepdims=True)
    log_total = highest[:, 0] + jnp.log(jnp.sum(jnp.exp(unnormalized_odds - highest), axis=1))
    columns = jnp.arange(relevance_matrix.shape[1], dtype=jnp.int32)
    correct_label = (columns[None, :] == matching_pair[:, None]).astype(jnp.float32)
    objective_value = log_total - jnp.sum(unnormalized_odds * correct_label, axis=1)
    probability_share = jnp.exp(unnormalized_odds - log_total[:, None])
    score_slope = OBJECTIVE_FACTOR * logit_multiplier * (probability_share - correct_label)
    return (objective_value, score_slope)


def query_weights(request_span, count):
    places = jnp.arange(count, dtype=jnp.int32)
    ones = jnp.where(places[None, :] < request_span[:, None], 1.0, 0.0).astype(jnp.float32)
    return ones / request_span[:, None].astype(jnp.float32)


def live_tokens(passage_span, count):
    places = jnp.arange(count, dtype=jnp.int32)
    return places[None, :] < passage_span[:, None]


def own_rows_pass(query_rows, own_weights, documents, live_all, pooling_steepness):
    pairs = own_weights.shape[0]
    features = query_rows.shape[1]
    total_pairs = documents.shape[0]
    group = math.gcd(total_pairs, max(1, 2048 // DLEN))
    blocks = total_pairs // group

    def block_similarity(start, count):
        docs_block = lax.dynamic_slice_in_dim(documents, start, count, 0).reshape(
            count * DLEN, features
        )
        live_block = lax.dynamic_slice_in_dim(live_all, start, count, 0)
        similarity = lax.dot_general(
            query_rows, docs_block, (((1,), (1,)), ((), ())), preferred_element_type=jnp.float32
        )
        return (similarity.reshape(pairs * QLEN, count, DLEN), live_block, docs_block)

    def forward_pass(index):
        similarity, live_block, _ = block_similarity(index * group, group)
        smooth, _ = pool_tokens(similarity, pooling_steepness, live_block)
        return jnp.sum(smooth.reshape(pairs, QLEN, group) * own_weights[:, :, None], axis=1)

    block_ids = jnp.arange(blocks, dtype=jnp.int32)
    relevance_matrix = lax.map(forward_pass, block_ids)
    relevance_matrix = jnp.transpose(relevance_matrix, (1, 0, 2)).reshape(pairs, total_pairs)
    return (relevance_matrix, block_similarity, group, block_ids)


def own_query_grads(
    query_rows, own_weights, score_slope, block_similarity, group, block_ids, pooling_steepness
):
    pairs = own_weights.shape[0]
    features = query_rows.shape[1]

    def gradient_block(start, count):
        similarity, live_block, docs_block = block_similarity(start, count)
        _, token_weight = pool_tokens(similarity, pooling_steepness, live_block)
        grad_block = lax.dynamic_slice_in_dim(score_slope, start, count, 1)
        coefficient = (own_weights[:, :, None] * grad_block[:, None, :]).reshape(
            pairs * QLEN, count
        )
        similarity_gradient = (coefficient[:, :, None] * token_weight).astype(jnp.bfloat16)
        return (similarity_gradient.reshape(pairs * QLEN, count * DLEN), docs_block)

    def query_step(carry, index):
        similarity_gradient, docs_block = gradient_block(index * group, group)
        return (
            carry + jnp.dot(similarity_gradient, docs_block, preferred_element_type=jnp.float32),
            None,
        )

    grad_queries, _ = lax.scan(
        query_step, jnp.zeros((pairs * QLEN, features), jnp.float32), block_ids
    )
    return (grad_queries, gradient_block)


def own_doc_pass(queries, doc_rows, weights_all, own_live, grad_columns, pooling_steepness):
    total_pairs = queries.shape[0]
    features = doc_rows.shape[1]
    pairs = own_live.shape[0]
    group = math.gcd(total_pairs, max(1, 1024 // QLEN))
    blocks = total_pairs // group

    def block_similarity(index):
        query_block = lax.dynamic_slice_in_dim(queries, index * group, group, 0).reshape(
            group * QLEN, features
        )
        similarity = lax.dot_general(
            query_block, doc_rows, (((1,), (1,)), ((), ())), preferred_element_type=jnp.float32
        )
        block_weight = lax.dynamic_slice_in_dim(weights_all, index * group, group, 0)
        return (similarity.reshape(group * QLEN, pairs, DLEN), block_weight, query_block)

    def backward(carry, index):
        similarity, block_weight, query_block = block_similarity(index)
        _, token_weight = pool_tokens(similarity, pooling_steepness, own_live)
        grad_block = lax.dynamic_slice_in_dim(grad_columns, index * group, group, 0)
        coefficient = (block_weight[:, :, None] * grad_block[:, None, :]).reshape(
            group * QLEN, pairs
        )
        similarity_gradient = (
            (coefficient[:, :, None] * token_weight)
            .astype(jnp.bfloat16)
            .reshape(group * QLEN, pairs * DLEN)
        )
        carry = carry + lax.dot_general(
            similarity_gradient,
            query_block,
            (((0,), (0,)), ((), ())),
            preferred_element_type=jnp.float32,
        )
        return (carry, None)

    block_ids = jnp.arange(blocks, dtype=jnp.int32)
    return (block_similarity, block_ids, group, backward)


def with_both(
    own_queries,
    own_docs,
    weights_all,
    live_all,
    selected_entry,
    first,
    pooling_steepness,
    logit_multiplier,
):
    pairs = own_queries.shape[0]
    features = own_queries.shape[2]
    queries, documents = (
        lax.all_gather(own_queries, "dp", axis=0, tiled=True),
        lax.all_gather(own_docs, "dp", axis=0, tiled=True),
    )
    query_rows = own_queries.reshape(pairs * QLEN, features)
    doc_rows = own_docs.reshape(pairs * DLEN, features)
    own_weights = lax.dynamic_slice_in_dim(weights_all, first, pairs, 0)
    own_live = lax.dynamic_slice_in_dim(live_all, first, pairs, 0)
    relevance_matrix, block_similarity, group, block_ids = own_rows_pass(
        query_rows, own_weights, documents, live_all, pooling_steepness
    )
    all_scores = lax.all_gather(relevance_matrix, "dp", axis=0, tiled=True)
    loss_all, grad_all = versus_term(all_scores, selected_entry, logit_multiplier)
    objective_value = lax.dynamic_slice_in_dim(loss_all, first, pairs, 0)
    grad_rows = lax.dynamic_slice_in_dim(grad_all, first, pairs, 0)
    grad_columns = lax.dynamic_slice_in_dim(grad_all, first, pairs, 1)
    grad_queries, _ = own_query_grads(
        query_rows, own_weights, grad_rows, block_similarity, group, block_ids, pooling_steepness
    )
    _, doc_block_ids, _, backward = own_doc_pass(
        queries, doc_rows, weights_all, own_live, grad_columns, pooling_steepness
    )
    grad_docs, _ = lax.scan(
        backward, jnp.zeros((pairs * DLEN, features), jnp.float32), doc_block_ids
    )
    return (
        grad_queries.reshape(pairs, QLEN, features),
        grad_docs.reshape(pairs, DLEN, features),
        objective_value,
    )


def local(
    latent_states,
    rescale_factor,
    embedding_matrix,
    request_span,
    passage_span,
    matching_pair,
    steepness_pair,
):
    full_proj = lax.all_gather(embedding_matrix, "section", axis=0, tiled=True)
    batch = lax.axis_index("section")
    pairs = latent_states.shape[1]
    length = latent_states.shape[2]
    width = latent_states.shape[3]
    first = lax.axis_index("dp") * pairs
    pooling_steepness = steepness_pair[0]
    logit_multiplier = steepness_pair[1]
    request_spans = lax.dynamic_index_in_dim(request_span, batch, 0, keepdims=False)
    passage_spans = lax.dynamic_index_in_dim(passage_span, batch, 0, keepdims=False)
    selected_entry = lax.dynamic_index_in_dim(matching_pair, batch, 0, keepdims=False)
    weights_all = query_weights(request_spans, QLEN)
    live_all = live_tokens(passage_spans, DLEN)
    flat_rows = latent_states.reshape(pairs * length, width)
    vectors, projected, inverse_length, inverse_rms = head_forward(
        flat_rows, rescale_factor, full_proj
    )
    vectors = vectors.reshape(pairs, length, -1)
    features = vectors.shape[2]
    own_queries = vectors[:, :QLEN]
    own_docs = vectors[:, QLEN:]
    grad_queries, grad_docs, objective_value = with_both(
        own_queries,
        own_docs,
        weights_all,
        live_all,
        selected_entry,
        first,
        pooling_steepness,
        logit_multiplier,
    )
    grad_vectors = jnp.concatenate([grad_queries, grad_docs], axis=1).reshape(
        pairs * length, features
    )
    grad_rows = head_backward(
        flat_rows, rescale_factor, full_proj, projected, inverse_length, inverse_rms, grad_vectors
    )
    return (grad_rows.reshape(1, pairs, length, width), objective_value[None, :])


def solution(mesh):
    return jax.shard_map(
        local,
        mesh=mesh,
        in_specs=(P("section", "dp", None, None), P(), P("section", None), P(), P(), P(), P()),
        out_specs=(P("section", "dp", None, None), P("section", "dp")),
        check_vma=False,
    )
```

profile of v0, /device:TPU:0, one launch (start us, length us, event | category | flops | bytes accessed | tf_op | source)
XLA Modules:
  0.0 135.8 jit_solution(408165753325786143)
XLA Ops:
  1.3 1.2 fusion.34
  2.5 1.3 fusion.36
  4.5 1.8 %fusion.2 = f32[4,96]{1,0:T(4,128)S(1)} fusion(bf16[1,4,96,2048]{3,2,1,0:T(8,128)(2,1)} %param.7), kind=kLoop, calls=%fused_computation.6 | loop fusion | flops 2358912 | bytes 1574400 | tf_op jit(solution)/shard_map/reduce_sum | solution.py:16
  9.0 8.8 %all_gather.12 = bf16[2048,128]{1,0:T(8,128)(2,1)S(1)} all-gather(bf16[512,128]{1,0:T(8,128)(2,1)} %param.9), channel_id=1, replica_groups=mesh['section'=4,'dp'=8] {'section'}, dimensions={0}, use_global_device_ids=true | all-gather | bytes 655360 | tf_op jit(solution)/shard_map/all_gather | solution.py:234
  17.8 1.1 fusion.4
  19.8 33.1 %all_gather.15 = bf16[32,32,128]{2,1,0:T(8,128)(2,1)} all-gather(bf16[4,32,128]{2,1,0:T(8,128)(2,1)S(1)} %slice.16), channel_id=1, replica_groups=mesh['section'=4,'dp'=8] {'dp'}, dimensions={0}, use_global_device_ids=true | all-gather | bytes 294912 | tf_op jit(solution)/shard_map/all_gather | solution.py:194
  52.9 31.2 %all_gather.13 = bf16[32,64,128]{2,1,0:T(8,128)(2,1)S(1)} all-gather(bf16[4,64,128]{2,1,0:T(8,128)(2,1)S(1)} %slice.17), channel_id=1, replica_groups=mesh['section'=4,'dp'=8] {'dp'}, dimensions={0}, use_global_device_ids=true | all-gather | bytes 589824 | tf_op jit(solution)/shard_map/all_gather | solution.py:195
  84.1 0.8 copy-done.2
  84.9 1.2 fusion.37
  86.3 1.3 add_divide_fusion
  87.6 0.8 div.62
  88.4 0.7 multiply_reduce_fusion.1
  89.1 0.8 copy.15
  89.9 26.1 %all-gather = f32[8,4,32]{2,1,0:T(4,128)S(1)} all-gather(f32[1,4,32]{2,1,0:T(4,128)S(1)} %bitcast.82), channel_id=1, replica_groups=mesh['section'=4,'dp'=8] {'dp'}, dimensions={0}, use_global_device_ids=true | all-gather | bytes 4608 | tf_op jit(solution)/shard_map/all_gather | solution.py:204
  116.0 0.7 fusion.33
  116.9 0.8 select_reduce_fusion
  119.8 0.8 mul.254
  121.3 0.7 broadcast_multiply_fusion.2
  122.0 1.1 multiply_convert_fusion
  123.9 3.2 %fusion.17 = f32[4,64,128]{2,1,0:T(8,128)} fusion(bf16[1024,128,1]{1,0,2:T(8,128)(2,1)} %bitcast.79, f32[1024,4]{0,1:T(4,128)S(1)} %broadcast_multiply_fusion.1, f32[]{:T(128)} %bitcast.4, pred[4,64]{1,0:T(4,128)(4,1)} %constant_dynamic-slice_fusion, bf16[4,96,128]{2,1,0:T(8,128)(2,1)S(1)} %bitcast.77), kind=kOutput, calls=%fused_computation.24 | convolution fusion | flops 135798912 | bytes 738304 | tf_op jit(solution)/shard_map/while/body/eval_jaxpr/dot_general | solution.py:169
  127.1 2.5 %copy.17 = bf16[128,32,64]{2,1,0:T(8,128)(2,1)} copy(bf16[128,32,64]{0,2,1:T(8,128)(2,1)S(1)} %copy-done.4) | data formatting | bytes 1048576 | tf_op jit(solution)/shard_map/while/body/eval_jaxpr/convert_element_type | solution.py:124
  129.6 2.0 %dot_general.32 = bf16[4,32,2048]{2,1,0:T(8,128)(2,1)S(1)} reshape(bf16[128,32,64]{2,1,0:T(8,128)(2,1)} %copy.17) | data formatting | bytes 1048576 | tf_op jit(solution)/shard_map/while/body/eval_jaxpr/dot_general | solution.py:130
  132.0 0.9 pad_maximum_fusion
  134.0 1.8 %fusion.7 = bf16[384,2048]{1,0:T(8,128)(2,1)} fusion(bf16[1,4,96,2048]{3,2,1,0:T(8,128)(2,1)S(1)} %copy-done.1, f32[384,2048]{1,0:T(8,128)S(1)} %get-tuple-element.78, f32[384]{0:T(512)S(1)} %broadcast_multiply_fusion.3, f32[384]{0:T(512)S(1)} %copy-done.6, f32[384]{0:T(512)S(1)} %rsqrt.23), kind=kLoop, calls=%fused_computation.11 | loop fusion | flops 4718592 | bytes 6296064 | tf_op jit(solution)/shard_map/convert_element_type | solution.py:48
  (46 shorter events, 9.6 us)
Async XLA Ops:
  0.6 0.7 copy-start
  0.6 17.2 %copy-start.1 = (bf16[1,4,96,2048]{3,2,1,0:T(8,128)(2,1)S(1)}, bf16[1,4,96,2048]{3,2,1,0:T(8,128)(2,1)}, u32[]{:S(2)}) copy-start(bf16[1,4,96,2048]{3,2,1,0:T(8,128)(2,1)} %param.7) | copy-start | bytes 4718596
  84.1 0.8 copy-start.2
  123.1 4.0 %copy-start.4 = (bf16[128,32,64]{0,2,1:T(8,128)(2,1)S(1)}, bf16[128,32,64]{0,2,1:T(8,128)(2,1)}, u32[]{:S(2)}) copy-start(bf16[128,32,64]{0,2,1:T(8,128)(2,1)} %multiply_convert_fusion) | copy-start | bytes 1572868
  123.9 7.7 %copy-start.3 = (bf16[32,64,128]{2,1,0:T(8,128)(2,1)S(1)}, bf16[32,64,128]{2,1,0:T(8,128)(2,1)}, u32[]{:S(2)}) copy-start(bf16[32,64,128]{2,1,0:T(8,128)(2,1)} %copy-done.2) | copy-start | bytes 1572868
  127.1 6.2 %copy-start.5 = (f32[2048]{0:T(1024)S(1)}, f32[2048]{0:T(1024)}, u32[]{:S(2)}) copy-start(f32[2048]{0:T(1024)} %param.8) | copy-start | bytes 24580
  132.9 1.1 copy-start.6
where the time goes:
time: 137 us; the launch traced here: 136 us
  blocking collectives  99.2 us (72%)
  other arithmetic  15 us (11%)
  local copies, waits for them, and re-layouts  14.1 us (10%)
  matrix products  6.05 us (4%)
  between operations  1.46 us (1%)
    all_gather x1, blocking collectives, with_both(): lax.all_gather(own_queries, 'dp', axis=0, tiled=True)  33.1 us
    all_gather x1, blocking collectives, with_both(): lax.all_gather(own_docs, 'dp', axis=0, tiled=True)  31.2 us
    all_gather x1, blocking collectives, with_both(): all_scores = lax.all_gather(relevance_matrix, 'dp', axis=0, tiled=True)  26.1 us
    all_gather x1, blocking collectives, local(): full_proj = lax.all_gather(embedding_matrix, 'section', axis=0, tiled=True)  8.84 us
    dot_general x1, matrix products, backward(): lax.dot_general(similarity_gradient, query_block, (((0,), (0,)), ((), ())...  3.16 us

commit v1 on v0

--- a/solution.py
+++ b/solution.py
@@ -231,7 +231,15 @@
     matching_pair,
     steepness_pair,
 ):
-    full_proj = lax.all_gather(embedding_matrix, "section", axis=0, tiled=True)
+    size = lax.axis_size("section")
+    held, pieces = (embedding_matrix, [embedding_matrix])
+    for _ in range(size - 1):
+        held = lax.ppermute(held, "section", [(i, (i + 1) % size) for i in range(size)])
+        pieces.insert(0, held)
+    row_of_blocks = jnp.concatenate(pieces, axis=0)
+    full_proj = jnp.roll(
+        row_of_blocks, (lax.axis_index("section") + 1) * embedding_matrix.shape[0], axis=0
+    )
     batch = lax.axis_index("section")
     pairs = latent_states.shape[1]
     length = latent_states.shape[2]

time: 137 us -> 121 us (0.88)
  local copies, waits for them, and re-layouts: 14.1 us -> 4.91 us
  blocking collectives: 99.2 us -> 91.4 us
  other arithmetic: 15 us -> 9.12 us
  waiting for transfers between devices: 0 us -> 5.11 us
  starting transfers between devices: 0 us -> 3 us
    all_gather x1 -> x0, blocking collectives: 8.84 us -> none  [local(): full_proj = lax.all_gather(embedding_matrix, 'section', axis=0, tiled=True)]
    ppermute x0 -> x3, waiting for transfers between devices: none -> 5.11 us  [local(): lax.ppermute(held, 'section', [(i, (i + 1) % size) for i in range(size)])]
    ppermute x0 -> x3, starting transfers between devices: none -> 3 us  [local(): lax.ppermute(held, 'section', [(i, (i + 1) % size) for i in range(size)])]
    mul x3, local copies, waits for them, and re-layouts: 2.12 us -> 0.27 us  [gradient_block(): own_weights[:, :, None] * grad_block[:, None, :]]
  transfers between devices with their start and end apart: 0 -> 3, of which waited for: 0 -> 3; matrix products, arithmetic and copies ran while one was open for 0% -> 4% of each run, Pallas kernels for 0% -> 0%
where the time goes in v1:
time: 121 us
  blocking collectives  91.4 us (76%)
  other arithmetic  9.12 us (8%)
  matrix products  5.4 us (4%)
  waiting for transfers between devices  5.11 us (4%)
  local copies, waits for them, and re-layouts  4.91 us (4%)
  starting transfers between devices  3 us (2%)
  between operations  1.61 us (1%)
    all_gather x1, blocking collectives, with_both(): lax.all_gather(own_queries, 'dp', axis=0, tiled=True)  34.1 us
    all_gather x1, blocking collectives, with_both(): lax.all_gather(own_docs, 'dp', axis=0, tiled=True)  31.2 us
    all_gather x1, blocking collectives, with_both(): all_scores = lax.all_gather(relevance_matrix, 'dp', axis=0, tiled=True)  26.1 us
    ppermute x3, waiting for transfers between devices, local(): lax.ppermute(held, 'section', [(i, (i + 1) % size) for i in range(size)])  5.11 us
    ppermute x3, starting transfers between devices, local(): lax.ppermute(held, 'section', [(i, (i + 1) % size) for i in range(size)])  3 us
    dot_general x1, matrix products, backward(): lax.dot_general(similarity_gradient, query_block, (((0,), (0,)), ((), ())...  2.54 us
  transfers between devices with their start and end apart: 3, of which 3 were waited for; matrix products, arithmetic and copies ran while one was open for 4% of the time, Pallas kernels for 0%

profile of v1, /device:TPU:0, one launch (start us, length us, event | category | flops | bytes accessed | tf_op | source)
XLA Modules:
  0.0 120.5 jit_solution(9145701686501613927)
XLA Ops:
  0.7 0.5 collective-permute-start
  1.2 1.8 %fusion.2 = f32[4,96]{1,0:T(4,128)S(1)} fusion(bf16[1,4,96,2048]{3,2,1,0:T(8,128)(2,1)} %param.7), kind=kLoop, calls=%fused_computation.6 | loop fusion | flops 2358912 | bytes 1574400 | tf_op jit(solution)/shard_map/reduce_sum | solution.py:16
  3.1 0.7 fusion.39
  3.9 1.8 %fusion.4 = bf16[384,2048]{1,0:T(8,128)(2,1)S(1)} fusion(bf16[1,4,96,2048]{3,2,1,0:T(8,128)(2,1)} %param.7, f32[2048]{0:T(1024)} %param.8, f32[384]{0:T(512)S(1)} %rsqrt.23), kind=kLoop, calls=%fused_computation.8 | loop fusion | flops 3145728 | bytes 3155456 | tf_op jit(solution)/shard_map/convert_element_type | solution.py:17
  6.0 2.5 %collective-permute-start.1 = (bf16[512,128]{1,0:T(8,128)(2,1)S(1)}, bf16[512,128]{1,0:T(8,128)(2,1)S(1)}, u32[]{:S(2)}, u32[]{:S(2)}) collective-permute-start(bf16[512,128]{1,0:T(8,128)(2,1)S(1)} %collective-permute-done), channel_id=1, source_target_pairs={{0,8},{8,16},{16,24},{24,0},{1,9},{9,17},{17,25},{25,1},{2,10},{10... | collective-permute-start | bytes 393224 | tf_op jit(solution)/shard_map/ppermute | solution.py:237
  8.4 0.6 fusion.41
  9.0 1.4 %collective-permute-done.1 = bf16[512,128]{1,0:T(8,128)(2,1)S(1)} collective-permute-done((bf16[512,128]{1,0:T(8,128)(2,1)S(1)}, bf16[512,128]{1,0:T(8,128)(2,1)S(1)}, u32[]{:S(2)}, u32[]{:S(2)}) %collective-permute-start.1) | collective-permute-done | bytes 131104 | tf_op jit(solution)/shard_map/ppermute | solution.py:237
  11.3 3.5 %collective-permute-done.2 = bf16[512,128]{1,0:T(8,128)(2,1)S(1)} collective-permute-done((bf16[512,128]{1,0:T(8,128)(2,1)S(1)}, bf16[512,128]{1,0:T(8,128)(2,1)S(1)}, u32[]{:S(2)}, u32[]{:S(2)}) %collective-permute-start.2) | collective-permute-done | bytes 131104 | tf_op jit(solution)/shard_map/ppermute | solution.py:237
  15.0 0.7 multiply_reduce_fusion
  15.9 34.1 %all_gather.11 = bf16[32,32,128]{2,1,0:T(8,128)(2,1)} all-gather(bf16[4,32,128]{2,1,0:T(8,128)(2,1)S(1)} %slice.16), channel_id=1, replica_groups=mesh['section'=4,'dp'=8] {'dp'}, dimensions={0}, use_global_device_ids=true | all-gather | bytes 294912 | tf_op jit(solution)/shard_map/all_gather | solution.py:194
  50.0 31.2 %all_gather.9 = bf16[32,64,128]{2,1,0:T(8,128)(2,1)S(1)} all-gather(bf16[4,64,128]{2,1,0:T(8,128)(2,1)S(1)} %slice.17), channel_id=1, replica_groups=mesh['section'=4,'dp'=8] {'dp'}, dimensions={0}, use_global_device_ids=true | all-gather | bytes 589824 | tf_op jit(solution)/shard_map/all_gather | solution.py:195
  81.1 1.2 %fusion.42 = (f32[128,32]{0,1:T(8,128)S(1)}, f32[128,32,64]{0,2,1:T(8,128)S(1)}) fusion(bf16[128,128,1]{1,0,2:T(8,128)(2,1)S(1)} %bitcast.76, bf16[32,64,128]{2,1,0:T(8,128)(2,1)S(1)} %all_gather.9, f32[]{:T(128)} %bitcast.4, pred[32,64]{1,0:T(8,128)(4,1)S(1)} %iota_compare_fusion.1), kind=kOutput, calls=%fused_computation.87 | convolution fusion | flops 67891200 | bytes 1624068 | tf_op jit(solution)/shard_map/while/body/eval_jaxpr/dot_general | solution.py:95
  82.6 0.7 add_divide_fusion
  83.5 26.1 %all-gather = f32[8,4,32]{2,1,0:T(4,128)S(1)} all-gather(f32[1,4,32]{2,1,0:T(4,128)S(1)} %bitcast.80), channel_id=1, replica_groups=mesh['section'=4,'dp'=8] {'dp'}, dimensions={0}, use_global_device_ids=true | all-gather | bytes 4608 | tf_op jit(solution)/shard_map/all_gather | solution.py:204
  109.6 0.7 fusion.38
  110.9 0.6 dynamic-slice_bitcast_fusion
  111.8 0.3 multiply_convert_fusion
  112.3 1.6 %copy.17 = bf16[128,32,64]{2,1,0:T(8,128)(2,1)S(1)} copy(bf16[128,32,64]{0,2,1:T(8,128)(2,1)S(1)} %multiply_convert_fusion) | data formatting | bytes 1048576 | tf_op jit(solution)/shard_map/while/body/eval_jaxpr/convert_element_type | solution.py:124
  113.9 0.8 dot_general.32
  114.7 0.3 fusion.47
  115.0 2.5 %fusion.17 = f32[4,64,128]{2,1,0:T(8,128)S(1)} fusion(bf16[1024,128,1]{1,0,2:T(8,128)(2,1)} %bitcast.77, f32[1024,4]{0,1:T(4,128)S(1)} %broadcast_multiply_fusion.1, f32[]{:T(128)} %bitcast.4, pred[4,64]{1,0:T(4,128)(4,1)S(1)} %constant_dynamic-slice_fusion, bf16[4,96,128]{2,1,0:T(8,128)(2,1)S(1)} %bitcast.75), kind=kOutput, calls=%fused_computation.24 | convolution fusion | flops 135798912 | bytes 738304 | tf_op jit(solution)/shard_map/while/body/eval_jaxpr/dot_general | solution.py:169
  117.6 0.2 fusion.23
  118.0 0.7 fusion.8
  118.7 1.8 %fusion.7 = bf16[384,2048]{1,0:T(8,128)(2,1)} fusion(bf16[1,4,96,2048]{3,2,1,0:T(8,128)(2,1)S(1)} %copy-done.1, f32[384,2048]{1,0:T(8,128)S(1)} %get-tuple-element.78, f32[384]{0:T(512)S(1)} %broadcast_multiply_fusion.3, f32[384]{0:T(512)S(1)} %multiply_multiply_fusion, f32[384]{0:T(512)S(1)} %rsqrt.23), kind=kLoop, calls=%fused_computation.11 | loop fusion | flops 4718592 | bytes 6296064 | tf_op jit(solution)/shard_map/convert_element_type | solution.py:48
  (55 shorter events, 2.6 us)
Async XLA Ops:
  0.6 2.5 %copy-start = (s32[4,32]{1,0:T(4,128)S(1)}, s32[4,32]{1,0:T(4,128)}, u32[]{:S(2)}) copy-start(s32[4,32]{1,0:T(4,128)} %param.11) | copy-start | bytes 1540
  0.6 14.3 %copy-start.2 = (bf16[512,128]{1,0:T(8,128)(2,1)S(1)}, bf16[512,128]{1,0:T(8,128)(2,1)}, u32[]{:S(2)}) copy-start(bf16[512,128]{1,0:T(8,128)(2,1)} %param.9) | copy-start | bytes 393220
  0.7 7.8 %copy-start.4 = (f32[2]{0:T(128)S(1)}, f32[2]{0:T(128)}, u32[]{:S(2)}) copy-start(f32[2]{0:T(128)} %param.13) | copy-start | bytes 28
  0.7 5.3 %collective-permute-start = (bf16[512,128]{1,0:T(8,128)(2,1)}, bf16[512,128]{1,0:T(8,128)(2,1)S(1)}, u32[]{:S(2)}, u32[]{:S(2)}) collective-permute-start(bf16[512,128]{1,0:T(8,128)(2,1)} %param.9), channel_id=1, source_target_pairs={{0,8},{8,16},{16,24},{24,0},{1,9},{9,17},{17,25},{25,1},{2,10},{10... | collective-permute-start | bytes 393224 | tf_op jit(solution)/shard_map/ppermute | solution.py:237
  6.0 4.5 %collective-permute-start.1 = (bf16[512,128]{1,0:T(8,128)(2,1)S(1)}, bf16[512,128]{1,0:T(8,128)(2,1)S(1)}, u32[]{:S(2)}, u32[]{:S(2)}) collective-permute-start(bf16[512,128]{1,0:T(8,128)(2,1)S(1)} %collective-permute-done), channel_id=1, source_target_pairs={{0,8},{8,16},{16,24},{24,0},{1,9},{9,17},{17,25},{25,1},{2,10},{10... | collective-permute-start | bytes 393224 | tf_op jit(solution)/shard_map/ppermute | solution.py:237
  10.4 4.4 %collective-permute-start.2 = (bf16[512,128]{1,0:T(8,128)(2,1)S(1)}, bf16[512,128]{1,0:T(8,128)(2,1)S(1)}, u32[]{:S(2)}, u32[]{:S(2)}) collective-permute-start(bf16[512,128]{1,0:T(8,128)(2,1)S(1)} %collective-permute-done.1), channel_id=1, source_target_pairs={{0,8},{8,16},{16,24},{24,0},{1,9},{9,17},{17,25},{25,1},{2,10},{10... | collective-permute-start | bytes 393224 | tf_op jit(solution)/shard_map/ppermute | solution.py:237
  115.0 3.0 %copy-start.1 = (bf16[1,4,96,2048]{3,2,1,0:T(8,128)(2,1)S(1)}, bf16[1,4,96,2048]{3,2,1,0:T(8,128)(2,1)}, u32[]{:S(2)}) copy-start(bf16[1,4,96,2048]{3,2,1,0:T(8,128)(2,1)} %param.7) | copy-start | bytes 4718596
  115.0 3.0 %copy-start.3 = (f32[2048]{0:T(1024)S(1)}, f32[2048]{0:T(1024)}, u32[]{:S(2)}) copy-start(f32[2048]{0:T(1024)} %param.8) | copy-start | bytes 24580
